TPU v7x, 32 devices: a whole 2x2x4 slice. The times are simulated.
32 devices in a mesh: pass: 16 (over z, y, core), voc: 2 (over x).
Axes of the slice: x: 2, y: 2, z: 4, core: 2. Of those that a mesh axis runs over, the one named last changes fastest.
Arguments:
- hidden: bfloat16 [512, 16, 768], P('pass'), may hold values from -6 to 6
- positions: int32 [512, 8], P('pass'), may hold values from 0 to 15
- passage_weight: float32 [512], P('pass'), may hold values from 0.4 to 2.5
- passage_counts: int32 [32], replicated, may hold values from 1 to 24, 512 in all
- passage_slot: int32 [512], replicated, may hold values from 0 to 511, each once
- head_weight: bfloat16 [768, 30720], P(None, 'voc'), may hold values from -0.21875 to 0.21875
- head_bias: float32 [30720], P('voc'), may hold values from -5 to 5
- queries: bfloat16 [32, 30720], P('pass', 'voc'), may hold values from -1 to 1
Outputs:
- scores: float32 [32, 32], P('pass')
- hidden_grad: bfloat16 [512, 16, 768], P('pass')
Inputs may be any that keep to these rules, and one draw needn't show every extreme that they name: `passage_slot`: each slot holds exactly one passage.
All inputs are finite; a program needn't handle non-finite values.
Results may differ from a plain program's by a relative error of at most 0.015.
Values may be sent and summed in bfloat16 or wider, within the bound.
No kernel may reach another device: no remote copies, remote signals or barrier semaphores. Data moves between devices by JAX's collectives and lax.ppermute only.
A program may use at most 128 MiB of HBM per device.

v0:
```python
import jax
import jax.numpy as jnp
from jax import lax
from jax.sharding import PartitionSpec as P

HIGH = lax.Precision.HIGHEST


def vocab_total(partial_value):
    return lax.psum(partial_value, "voc")


def score_gradient(scores, owned, doc_total):
    query_first = lax.axis_index("pass") * owned
    rows = query_first + jnp.arange(owned, dtype=jnp.int32)
    target = (jnp.arange(doc_total, dtype=jnp.int32)[None, :] == rows[:, None]).astype(jnp.float32)
    prob = jax.nn.softmax(scores, axis=1)
    return (prob - target) / doc_total


def on_device(
    hidden, positions, passage_weight, passage_counts, passage_slot, head_weight, head_bias, queries
):
    count = hidden.shape[0]
    seq_len = hidden.shape[1]
    width = hidden.shape[2]
    picks = positions.shape[1]
    total = passage_slot.shape[0]
    doc_total = passage_counts.shape[0]
    owned = queries.shape[0]
    vocab_local = head_weight.shape[1]
    ends = jnp.cumsum(passage_counts)
    order = jnp.arange(total, dtype=jnp.int32)
    doc_order = jnp.sum((ends[None, :] <= order[:, None]).astype(jnp.int32), axis=1)
    local_slot = lax.axis_index("pass") * count + jnp.arange(count, dtype=jnp.int32)
    matched = passage_slot[None, :] == local_slot[:, None]
    doc_local = jnp.sum(jnp.where(matched, doc_order[None, :], 0), axis=1)
    mixing = jnp.where(
        doc_local[None, :] == jnp.arange(doc_total, dtype=jnp.int32)[:, None],
        passage_weight[None, :],
        jnp.float32(0.0),
    )
    picked = jax.vmap(lambda h, p: h[p])(hidden, positions).reshape(-1, width)
    logits = jnp.dot(picked, head_weight, preferred_element_type=jnp.float32) + head_bias
    active = jnp.log1p(jnp.maximum(logits, 0.0))
    rep = active.reshape(count, picks, vocab_local).sum(axis=1).astype(jnp.bfloat16)
    all_queries = lax.all_gather(queries, "pass", axis=0, tiled=True)
    paired = lax.dot_general(
        all_queries, rep, (((1,), (1,)), ((), ())), preferred_element_type=jnp.float32
    )
    parts = lax.dot_general(paired, mixing, (((1,), (1,)), ((), ())), precision=HIGH)
    scores = vocab_total(lax.psum_scatter(parts, "pass", scatter_dimension=0, tiled=True))
    dscore = score_gradient(scores, owned, doc_total)
    all_dscore = lax.all_gather(dscore, "pass", axis=0, tiled=True)
    per_query = lax.dot_general(mixing, all_dscore, (((0,), (1,)), ((), ())), precision=HIGH)
    drep = jnp.dot(per_query, all_queries.astype(jnp.float32), precision=HIGH)
    shaped = logits.reshape(count, picks, vocab_local)
    growth = 1.0 + jnp.maximum(shaped, 0.0)
    dlogits = jnp.where(shaped > 0, drep[:, None, :] / growth, jnp.float32(0.0)).astype(
        jnp.bfloat16
    )
    token_part = lax.dot_general(
        dlogits.reshape(-1, vocab_local),
        head_weight,
        (((1,), (1,)), ((), ())),
        preferred_element_type=jnp.float32,
    )
    dpicked = lax.psum(token_part.astype(jnp.bfloat16), "voc").astype(jnp.float32)
    onehot = (positions[:, :, None] == jnp.arange(seq_len, dtype=jnp.int32)[None, None, :]).astype(
        jnp.float32
    )
    hidden_grad = jnp.einsum(
        "bps,bpd->bsd", onehot, dpicked.reshape(count, picks, width), precision=HIGH
    )
    return (scores, hidden_grad.astype(jnp.bfloat16))


def solution(mesh):
    placed = (
        P("pass", None, None),
        P("pass", None),
        P("pass"),
        P(),
        P(),
        P(None, "voc"),
        P("voc"),
        P("pass", "voc"),
    )
    return jax.shard_map(
        on_device,
        mesh=mesh,
        in_specs=placed,
        out_specs=(P("pass", None), P("pass", None, None)),
        check_vma=False,
    )
```

profile of v0, /device:TPU:0, one launch (start us, length us, event | category | flops | bytes accessed | tf_op | source)
XLA Modules:
  0.0 201.1 jit_solution(16383369175153553843)
XLA Ops:
  7.2 0.0 copy-start
  7.2 0.0 all-reduce.3.cloned.1.call-start
  7.2 0.8 fusion.26
  8.0 0.1 copy.18
  8.1 0.1 reshape.62
  8.2 26.2 %all-gather = bf16[16,2,15360]{2,1,0:T(2,128)(2,1)S(1)} all-gather(bf16[1,2,15360]{2,1,0:T(2,128)(2,1)} %bitcast.38), channel_id=1, replica_groups=mesh['pass'=16,'voc'=2] {'pass'}, dimensions={0}, use_global_device_ids=true | all-gather | bytes 1044480 | tf_op jit(solution)/shard_map/all_gather | solution.py:47
  34.4 0.4 reshape.75
  34.8 0.7 copy.19
  35.5 0.1 reduce-window.8
  35.6 0.1 reduce
  35.7 0.1 convert_reduce_fusion
  35.8 0.0 copy-done
  35.8 2.4 %gather_fusion = bf16[256,768]{1,0:T(8,128)(2,1)S(1)} fusion(bf16[32,16,768]{2,1,0:T(8,128)(2,1)S(1)} %copy-done, s32[256]{0:T(256)S(1)} %reshape.62), kind=kCustom, calls=%fused_computation | custom fusion | bytes 788480 | tf_op jit(solution)/shard_map/vmap()/gather | solution.py:43
  38.2 0.0 copy-start.4
  38.2 0.0 copy-start.3
  38.3 0.0 copy-start.5
  38.3 27.2 %bitcast_reduce_fusion = (bf16[32,15360]{1,0:T(8,128)(2,1)S(1)}, f32[256,15360]{1,0:T(8,128)}) fusion(f32[15360]{0:T(1024)} %param.14, bf16[256,768]{1,0:T(8,128)(2,1)S(1)} %gather_fusion, bf16[768,15360]{1,0:T(8,128)(2,1)} %param.13), kind=kOutput, calls=%fused_computation.5 | convolution fusion | flops 6051102720 | bytes 40759296 | tf_op jit(solution)/shard_map/dot_general | solution.py:44
  65.5 0.4 fusion.33
  65.9 0.0 copy-done.4
  65.9 0.2 select_reduce_fusion
  66.1 0.0 copy-done.3
  66.1 0.2 fusion.15
  66.3 57.8 %all-reduce = f32[32,32]{1,0:T(8,128)S(1)} all-reduce(f32[32,32]{1,0:T(8,128)S(1)} %fusion.15), channel_id=2, replica_groups=mesh['pass'=16,'voc'=2] {'pass'}, use_global_device_ids=true, to_apply=%region_4.5.clone | all-reduce | flops 1024 | bytes 8192
  124.1 0.0 copy-done.5
  124.2 0.6 dynamic-slice
  125.4 4.9 %psum.14 = f32[2,32]{1,0:T(2,128)S(1)} all-reduce(f32[2,32]{1,0:T(2,128)S(1)} %constant_dynamic-slice_fusion), channel_id=1, replica_groups=mesh['pass'=16,'voc'=2] {'voc'}, use_global_device_ids=true, to_apply=%region_5.6 | all-reduce | flops 64 | bytes 512 | tf_op jit(solution)/shard_map/psum | solution.py:10
  130.3 0.0 copy-start.2
  130.3 0.1 reduce_max.9
  130.5 0.2 fusion.27
  130.6 0.1 multiply_bitcast_fusion
  130.7 17.3 %all-gather.1 = f32[16,2,32]{2,1,0:T(2,128)S(1)} all-gather(f32[1,2,32]{2,1,0:T(2,128)S(1)} %multiply_bitcast_fusion), channel_id=1, replica_groups=mesh['pass'=16,'voc'=2] {'pass'}, dimensions={0}, use_global_device_ids=true | all-gather | bytes 4352 | tf_op jit(solution)/shard_map/all_gather | solution.py:54
  148.1 0.2 fusion.13
  148.3 2.2 %fusion.32 = f32[32,15360]{1,0:T(8,128)} fusion(f32[32,32]{1,0:T(8,128)S(1)} %fusion.13, bf16[32,15360]{1,0:T(8,128)(2,1)S(1)} %reshape.75), kind=kOutput, calls=%fused_computation.45 | convolution fusion | flops 188743680 | bytes 2953216 | tf_op jit(solution)/shard_map/dot_general | solution.py:56
  150.5 0.0 copy-start.1
  150.5 16.6 %fusion.7 = bf16[32,8,768]{2,1,0:T(8,128)(2,1)} fusion(bf16[768,15360]{1,0:T(8,128)(2,1)} %param.13, f32[256,15360]{1,0:T(8,128)} %get-tuple-element.3, f32[32,15360]{1,0:T(8,128)} %fusion.32), kind=kOutput, calls=%fused_computation.9 | convolution fusion | flops 6063587328 | bytes 41680896 | tf_op jit(solution)/shard_map/dot_general | solution.py:62
  167.0 0.0 copy-done.2
  167.0 0.0 all-reduce.3.cloned.1.call-update
  167.1 0.0 copy-done.1
  167.1 0.1 copy.20
  167.1 24.5 %all-reduce.3.cloned.1.call-done = bf16[32,8,768]{2,1,0:T(8,128)(2,1)} async-done(((bf16[32,8,768]{2,1,0:T(8,128)(2,1)}), bf16[32,8,768]{2,1,0:T(8,128)(2,1)}) %all-reduce.3.cloned.1.call-update) | async-done | bytes 393232 | tf_op jit(solution)/shard_map/psum | solution.py:68
  191.7 2.6 %convolution_convert_fusion = bf16[32,16,768]{2,1,0:T(8,128)(2,1)} fusion(bf16[32,8,768]{2,1,0:T(8,128)(2,1)} %all-reduce.3.cloned.1.call-done, s32[32,8]{1,0:T(8,128)S(1)} %copy.20), kind=kOutput, calls=%fused_computation.7 | convolution fusion | flops 6688768 | bytes 1180672 | tf_op jit(solution)/shard_map/bps,bpd->bsd/dot_general | solution.py:72
  (3 shorter events, 0.0 us)
Async XLA Ops:
  7.2 28.6 %copy-start = (bf16[32,16,768]{2,1,0:T(8,128)(2,1)S(1)}, bf16[32,16,768]{2,1,0:T(8,128)(2,1)}, u32[]{:S(2)}) copy-start(bf16[32,16,768]{2,1,0:T(8,128)(2,1)} %param.8) | copy-start | bytes 2359300
  7.2 184.5 %all-reduce.3.cloned.1.call-start = ((), (), s32[]{:S(2)}) async-start(), calls=%async_computation | async-start | bytes 786432 | tf_op jit(solution)/shard_map/psum | solution.py:68
  38.2 27.7 %copy-start.4 = (s32[512]{0:T(512)S(1)}, s32[512]{0:T(512)}, u32[]{:S(2)}) copy-start(s32[512]{0:T(512)} %param.12) | copy-start | bytes 6148
  38.2 27.9 %copy-start.3 = (f32[32]{0:T(128)S(1)}, f32[32]{0:T(128)}, u32[]{:S(2)}) copy-start(f32[32]{0:T(128)} %param.10) | copy-start | bytes 388
  38.3 85.9 %copy-start.5 = (u32[32]{0:T(128)S(1)}, u32[32]{0:T(128)}, u32[]{:S(2)}) copy-start(u32[32]{0:T(128)} %constant.46) | copy-start | bytes 388
  130.3 36.7 %copy-start.2 = (f32[2,32]{1,0:T(2,128)}, f32[2,32]{1,0:T(2,128)S(1)}, u32[]{:S(2)}) copy-start(f32[2,32]{1,0:T(2,128)S(1)} %psum.14) | copy-start | bytes 772
  150.5 16.6 %copy-start.1 = (s32[32,8]{0,1:T(8,128)S(1)}, s32[32,8]{0,1:T(8,128)}, u32[]{:S(2)}) copy-start(s32[32,8]{0,1:T(8,128)} %param.9) | copy-start | bytes 3076
Sparse Core Ops, SparseCore 0:
  167.2 24.4 all-reduce.2
where the time goes:
time: 201 us
  blocking collectives  106 us (53%)
  matrix products  49.4 us (25%)
  waiting for transfers between devices  24.5 us (12%)
  between operations  14.8 us (7%)
  local copies, waits for them, and re-layouts  4.4 us (2%)
    unnamed x1, blocking collectives  57.8 us
    dot_general x1, matrix products, on_device(): jnp.dot(picked, head_weight, preferred_element_type=jnp.float32) + head_bias  27.2 us
    all_gather x1, blocking collectives, on_device(): all_queries = lax.all_gather(queries, 'pass', axis=0, tiled=True)  26.2 us
    psum x1, waiting for transfers between devices, on_device(): lax.psum(token_part.astype(jnp.bfloat16), 'voc').astype(jnp.float32)  24.5 us
    all_gather x1, blocking collectives, on_device(): all_dscore = lax.all_gather(dscore, 'pass', axis=0, tiled=True)  17.3 us
    dot_general x1, matrix products, on_device(): lax.dot_general(dlogits.reshape(-1, vocab_local), head_weight, (((1,), (1...  16.6 us
    psum x1, blocking collectives, vocab_total(): return lax.psum(partial_value, 'voc')  4.93 us
  transfers between devices with their start and end apart: 1, of which 1 were waited for; matrix products, arithmetic and copies ran while one was open for 0% of the time, Pallas kernels for 0%

commit v1 on v0

--- a/solution.py
+++ b/solution.py
@@ -51,7 +51,14 @@
     parts = lax.dot_general(paired, mixing, (((1,), (1,)), ((), ())), precision=HIGH)
     scores = vocab_total(lax.psum_scatter(parts, "pass", scatter_dimension=0, tiled=True))
     dscore = score_gradient(scores, owned, doc_total)
-    all_dscore = lax.all_gather(dscore, "pass", axis=0, tiled=True)
+    x = dscore
+    ways, here, lap = (lax.axis_size("pass"), lax.axis_index("pass"), x.shape[0])
+    shape = [n * ways if d == 0 else n for d, n in enumerate(x.shape)]
+    full = lax.dynamic_update_slice_in_dim(jnp.zeros(shape, x.dtype), x, here * lap, axis=0)
+    for far in range(1, ways):
+        x = lax.ppermute(x, "pass", [(d, (d + 1) % ways) for d in range(ways)])
+        full = lax.dynamic_update_slice_in_dim(full, x, (here - far) % ways * lap, axis=0)
+    all_dscore = full
     per_query = lax.dot_general(mixing, all_dscore, (((0,), (1,)), ((), ())), precision=HIGH)
     drep = jnp.dot(per_query, all_queries.astype(jnp.float32), precision=HIGH)
     shaped = logits.reshape(count, picks, vocab_local)

time: 201 us -> 267 us (1.33)
  waiting for transfers between devices: 24.5 us -> 108 us
  blocking collectives: 106 us -> 89 us
    ppermute x0 -> x15, waiting for transfers between devices: none -> 85 us  [on_device(): x = lax.ppermute(x, 'pass', [(d, (d + 1) % ways) for d in range(ways)])]
    all_gather x1 -> x0, blocking collectives: 17.3 us -> none  [on_device(): all_dscore = lax.all_gather(dscore, 'pass', axis=0, tiled=True)]
  transfers between devices with their start and end apart: 1 -> 16, of which waited for: 1 -> 16; matrix products, arithmetic and copies ran while one was open for 0% -> 0% of each run, Pallas kernels for 0% -> 0%
where the time goes in v1:
time: 267 us; the launch traced here: 266 us
  waiting for transfers between devices  108 us (40%)
  blocking collectives  89 us (33%)
  matrix products  47.8 us (18%)
  between operations  15.2 us (6%)
  local copies, waits for them, and re-layouts  4.51 us (2%)
    ppermute x15, waiting for transfers between devices, on_device(): x = lax.ppermute(x, 'pass', [(d, (d + 1) % ways) for d in range(ways)])  85 us
    unnamed x1, blocking collectives  57.8 us
    dot_general x1, matrix products, on_device(): jnp.dot(picked, head_weight, preferred_element_type=jnp.float32) + head_bias  27.4 us
    all_gather x1, blocking collectives, on_device(): all_queries = lax.all_gather(queries, 'pass', axis=0, tiled=True)  26.2 us
    psum x1, waiting for transfers between devices, on_device(): lax.psum(token_part.astype(jnp.bfloat16), 'voc').astype(jnp.float32)  23.1 us
    dot_general x1, matrix products, on_device(): lax.dot_general(dlogits.reshape(-1, vocab_local), head_weight, (((1,), (1...  16.1 us
  transfers between devices with their start and end apart: 16, of which 16 were waited for; matrix products, arithmetic and copies ran while one was open for 0% of the time, Pallas kernels for 0%

profile of v1, /device:TPU:0, one launch (start us, length us, event | category | flops | bytes accessed | tf_op | source)
XLA Modules:
  0.0 266.3 jit_solution(13825186493736311001)
XLA Ops:
  7.2 0.0 copy-start
  7.2 0.0 all-reduce.3.cloned.1.call-start
  7.2 0.8 fusion.26
  8.0 0.1 copy.18
  8.1 0.1 reshape.62
  8.2 26.2 %all-gather = bf16[16,2,15360]{2,1,0:T(2,128)(2,1)S(1)} all-gather(bf16[1,2,15360]{2,1,0:T(2,128)(2,1)} %bitcast.34), channel_id=1, replica_groups=mesh['pass'=16,'voc'=2] {'pass'}, dimensions={0}, use_global_device_ids=true | all-gather | bytes 1044480 | tf_op jit(solution)/shard_map/all_gather | solution.py:47
  34.4 0.4 reshape.75
  34.8 0.7 copy.19
  35.5 0.1 reduce-window.8
  35.6 0.1 reduce
  35.7 0.1 convert_reduce_fusion
  35.8 2.4 gather_fusion
  38.2 0.0 copy-start.4
  38.3 0.0 copy-start.3
  38.3 0.0 copy-start.5
  38.3 27.4 %bitcast_reduce_fusion = (bf16[32,15360]{1,0:T(8,128)(2,1)S(1)}, f32[256,15360]{1,0:T(8,128)}) fusion(f32[15360]{0:T(1024)} %param.14, bf16[256,768]{1,0:T(8,128)(2,1)S(1)} %gather_fusion, bf16[768,15360]{1,0:T(8,128)(2,1)} %param.13), kind=kOutput, calls=%fused_computation.5 | convolution fusion | flops 6051102720 | bytes 40759296 | tf_op jit(solution)/shard_map/dot_general | solution.py:44
  65.7 0.4 fusion.35
  66.1 0.2 select_reduce_fusion
  66.3 0.0 copy-done.3
  66.3 0.2 fusion.15
  66.5 57.8 %all-reduce = f32[32,32]{1,0:T(8,128)S(1)} all-reduce(f32[32,32]{1,0:T(8,128)S(1)} %fusion.15), channel_id=2, replica_groups=mesh['pass'=16,'voc'=2] {'pass'}, use_global_device_ids=true, to_apply=%region_4.5.clone | all-reduce | flops 1024 | bytes 8192
  124.4 0.6 dynamic-slice
  125.6 4.9 %psum.14 = f32[2,32]{1,0:T(2,128)S(1)} all-reduce(f32[2,32]{1,0:T(2,128)S(1)} %constant_dynamic-slice_fusion), channel_id=1, replica_groups=mesh['pass'=16,'voc'=2] {'voc'}, use_global_device_ids=true, to_apply=%region_5.6 | all-reduce | flops 64 | bytes 512 | tf_op jit(solution)/shard_map/psum | solution.py:10
  130.5 0.1 reduce_max.9
  130.7 0.2 fusion.28
  130.9 0.1 constant_dynamic-update-slice_fusion.15
  131.0 0.0 collective-permute-start
  131.3 5.4 %collective-permute-done = f32[2,32]{1,0:T(2,128)S(1)} collective-permute-done((f32[2,32]{1,0:T(2,128)S(1)}, f32[2,32]{1,0:T(2,128)S(1)}, u32[]{:S(2)}, u32[]{:S(2)}) %collective-permute-start) | collective-permute-done | bytes 288 | tf_op jit(solution)/shard_map/ppermute | solution.py:59
  136.7 0.0 collective-permute-start.1
  136.7 5.7 %collective-permute-done.1 = f32[2,32]{1,0:T(2,128)S(1)} collective-permute-done((f32[2,32]{1,0:T(2,128)S(1)}, f32[2,32]{1,0:T(2,128)S(1)}, u32[]{:S(2)}, u32[]{:S(2)}) %collective-permute-start.1) | collective-permute-done | bytes 288 | tf_op jit(solution)/shard_map/ppermute | solution.py:59
  142.3 0.0 collective-permute-start.2
  142.4 5.7 %collective-permute-done.2 = f32[2,32]{1,0:T(2,128)S(1)} collective-permute-done((f32[2,32]{1,0:T(2,128)S(1)}, f32[2,32]{1,0:T(2,128)S(1)}, u32[]{:S(2)}, u32[]{:S(2)}) %collective-permute-start.2) | collective-permute-done | bytes 288 | tf_op jit(solution)/shard_map/ppermute | solution.py:59
  148.0 0.0 collective-permute-start.3
  148.1 5.7 %collective-permute-done.3 = f32[2,32]{1,0:T(2,128)S(1)} collective-permute-done((f32[2,32]{1,0:T(2,128)S(1)}, f32[2,32]{1,0:T(2,128)S(1)}, u32[]{:S(2)}, u32[]{:S(2)}) %collective-permute-start.3) | collective-permute-done | bytes 288 | tf_op jit(solution)/shard_map/ppermute | solution.py:59
  153.7 0.0 collective-permute-start.4
  153.8 5.7 %collective-permute-done.4 = f32[2,32]{1,0:T(2,128)S(1)} collective-permute-done((f32[2,32]{1,0:T(2,128)S(1)}, f32[2,32]{1,0:T(2,128)S(1)}, u32[]{:S(2)}, u32[]{:S(2)}) %collective-permute-start.4) | collective-permute-done | bytes 288 | tf_op jit(solution)/shard_map/ppermute | solution.py:59
  159.4 0.0 collective-permute-start.5
  159.5 5.7 %collective-permute-done.5 = f32[2,32]{1,0:T(2,128)S(1)} collective-permute-done((f32[2,32]{1,0:T(2,128)S(1)}, f32[2,32]{1,0:T(2,128)S(1)}, u32[]{:S(2)}, u32[]{:S(2)}) %collective-permute-start.5) | collective-permute-done | bytes 288 | tf_op jit(solution)/shard_map/ppermute | solution.py:59
  165.1 0.0 collective-permute-start.6
  165.1 5.7 %collective-permute-done.6 = f32[2,32]{1,0:T(2,128)S(1)} collective-permute-done((f32[2,32]{1,0:T(2,128)S(1)}, f32[2,32]{1,0:T(2,128)S(1)}, u32[]{:S(2)}, u32[]{:S(2)}) %collective-permute-start.6) | collective-permute-done | bytes 288 | tf_op jit(solution)/shard_map/ppermute | solution.py:59
  170.8 0.0 collective-permute-start.7
  170.8 5.7 %collective-permute-done.7 = f32[2,32]{1,0:T(2,128)S(1)} collective-permute-done((f32[2,32]{1,0:T(2,128)S(1)}, f32[2,32]{1,0:T(2,128)S(1)}, u32[]{:S(2)}, u32[]{:S(2)}) %collective-permute-start.7) | collective-permute-done | bytes 288 | tf_op jit(solution)/shard_map/ppermute | solution.py:59
  176.5 0.0 collective-permute-start.8
  176.5 5.7 %collective-permute-done.8 = f32[2,32]{1,0:T(2,128)S(1)} collective-permute-done((f32[2,32]{1,0:T(2,128)S(1)}, f32[2,32]{1,0:T(2,128)S(1)}, u32[]{:S(2)}, u32[]{:S(2)}) %collective-permute-start.8) | collective-permute-done | bytes 288 | tf_op jit(solution)/shard_map/ppermute | solution.py:59
  182.2 0.0 collective-permute-start.9
  182.2 5.7 %collective-permute-done.9 = f32[2,32]{1,0:T(2,128)S(1)} collective-permute-done((f32[2,32]{1,0:T(2,128)S(1)}, f32[2,32]{1,0:T(2,128)S(1)}, u32[]{:S(2)}, u32[]{:S(2)}) %collective-permute-start.9) | collective-permute-done | bytes 288 | tf_op jit(solution)/shard_map/ppermute | solution.py:59
  187.9 0.0 collective-permute-start.10
  187.9 5.7 %collective-permute-done.10 = f32[2,32]{1,0:T(2,128)S(1)} collective-permute-done((f32[2,32]{1,0:T(2,128)S(1)}, f32[2,32]{1,0:T(2,128)S(1)}, u32[]{:S(2)}, u32[]{:S(2)}) %collective-permute-start.10) | collective-permute-done | bytes 288 | tf_op jit(solution)/shard_map/ppermute | solution.py:59
  193.6 0.0 collective-permute-start.11
  193.6 5.7 %collective-permute-done.11 = f32[2,32]{1,0:T(2,128)S(1)} collective-permute-done((f32[2,32]{1,0:T(2,128)S(1)}, f32[2,32]{1,0:T(2,128)S(1)}, u32[]{:S(2)}, u32[]{:S(2)}) %collective-permute-start.11) | collective-permute-done | bytes 288 | tf_op jit(solution)/shard_map/ppermute | solution.py:59
  199.3 0.0 collective-permute-start.12
  199.3 5.7 %collective-permute-done.12 = f32[2,32]{1,0:T(2,128)S(1)} collective-permute-done((f32[2,32]{1,0:T(2,128)S(1)}, f32[2,32]{1,0:T(2,128)S(1)}, u32[]{:S(2)}, u32[]{:S(2)}) %collective-permute-start.12) | collective-permute-done | bytes 288 | tf_op jit(solution)/shard_map/ppermute | solution.py:59
  205.0 0.0 collective-permute-start.13
  205.0 5.7 %collective-permute-done.13 = f32[2,32]{1,0:T(2,128)S(1)} collective-permute-done((f32[2,32]{1,0:T(2,128)S(1)}, f32[2,32]{1,0:T(2,128)S(1)}, u32[]{:S(2)}, u32[]{:S(2)}) %collective-permute-start.13) | collective-permute-done | bytes 288 | tf_op jit(solution)/shard_map/ppermute | solution.py:59
  210.7 0.0 collective-permute-start.14
  210.7 5.7 %collective-permute-done.14 = f32[2,32]{1,0:T(2,128)S(1)} collective-permute-done((f32[2,32]{1,0:T(2,128)S(1)}, f32[2,32]{1,0:T(2,128)S(1)}, u32[]{:S(2)}, u32[]{:S(2)}) %collective-permute-start.14) | collective-permute-done | bytes 288 | tf_op jit(solution)/shard_map/ppermute | solution.py:59
  216.4 0.2 fusion.13
  216.6 0.9 fusion.34
  217.5 0.0 copy-start.1
  217.6 16.1 %fusion.7 = bf16[32,8,768]{2,1,0:T(8,128)(2,1)} fusion(bf16[768,15360]{1,0:T(8,128)(2,1)} %param.13, f32[256,15360]{1,0:T(8,128)} %get-tuple-element.5, f32[32,15360]{1,0:T(8,128)S(1)} %fusion.34), kind=kOutput, calls=%fused_computation.9 | convolution fusion | flops 6063587328 | bytes 41680896 | tf_op jit(solution)/shard_map/dot_general | solution.py:69
  233.7 0.0 all-reduce.3.cloned.1.call-update
  233.7 0.1 copy.20
  233.8 23.1 %all-reduce.3.cloned.1.call-done = bf16[32,8,768]{2,1,0:T(8,128)(2,1)} async-done(((bf16[32,8,768]{2,1,0:T(8,128)(2,1)}), bf16[32,8,768]{2,1,0:T(8,128)(2,1)}) %all-reduce.3.cloned.1.call-update) | async-done | bytes 393232 | tf_op jit(solution)/shard_map/psum | solution.py:75
  256.9 2.6 convolution_convert_fusion
  (25 shorter events, 0.1 us)
Async XLA Ops:
  7.2 28.6 %copy-start = (bf16[32,16,768]{2,1,0:T(8,128)(2,1)S(1)}, bf16[32,16,768]{2,1,0:T(8,128)(2,1)}, u32[]{:S(2)}) copy-start(bf16[32,16,768]{2,1,0:T(8,128)(2,1)} %param.8) | copy-start | bytes 2359300
  7.2 249.7 %all-reduce.3.cloned.1.call-start = ((), (), s32[]{:S(2)}) async-start(), calls=%async_computation | async-start | bytes 786432 | tf_op jit(solution)/shard_map/psum | solution.py:75
  38.2 27.9 %copy-start.4 = (s32[512]{0:T(512)S(1)}, s32[512]{0:T(512)}, u32[]{:S(2)}) copy-start(s32[512]{0:T(512)} %param.12) | copy-start | bytes 6148
  38.3 28.1 %copy-start.3 = (f32[32]{0:T(128)S(1)}, f32[32]{0:T(128)}, u32[]{:S(2)}) copy-start(f32[32]{0:T(128)} %param.10) | copy-start | bytes 388
  38.3 86.1 %copy-start.5 = (u32[32]{0:T(128)S(1)}, u32[32]{0:T(128)}, u32[]{:S(2)}) copy-start(u32[32]{0:T(128)} %constant.158) | copy-start | bytes 388
  130.5 103.1 %copy-start.2 = (f32[2,32]{1,0:T(2,128)}, f32[2,32]{1,0:T(2,128)S(1)}, u32[]{:S(2)}) copy-start(f32[2,32]{1,0:T(2,128)S(1)} %psum.14) | copy-start | bytes 772
  131.0 5.7 %collective-permute-start = (f32[2,32]{1,0:T(2,128)S(1)}, f32[2,32]{1,0:T(2,128)S(1)}, u32[]{:S(2)}, u32[]{:S(2)}) collective-permute-start(f32[2,32]{1,0:T(2,128)S(1)} %get-tuple-element.3), channel_id=1, source_target_pairs={{0,2},{2,4},{4,6},{6,8},{8,10},{10,12},{12,14},{14,16},{16,18},{18... | collective-permute-start | bytes 776 | tf_op jit(solution)/shard_map/ppermute | solution.py:59
  136.7 5.7 %collective-permute-start.1 = (f32[2,32]{1,0:T(2,128)S(1)}, f32[2,32]{1,0:T(2,128)S(1)}, u32[]{:S(2)}, u32[]{:S(2)}) collective-permute-start(f32[2,32]{1,0:T(2,128)S(1)} %collective-permute-done), channel_id=1, source_target_pairs={{0,2},{2,4},{4,6},{6,8},{8,10},{10,12},{12,14},{14,16},{16,18},{18... | collective-permute-start | bytes 776 | tf_op jit(solution)/shard_map/ppermute | solution.py:59
  142.3 5.7 %collective-permute-start.2 = (f32[2,32]{1,0:T(2,128)S(1)}, f32[2,32]{1,0:T(2,128)S(1)}, u32[]{:S(2)}, u32[]{:S(2)}) collective-permute-start(f32[2,32]{1,0:T(2,128)S(1)} %collective-permute-done.1), channel_id=1, source_target_pairs={{0,2},{2,4},{4,6},{6,8},{8,10},{10,12},{12,14},{14,16},{16,18},{18... | collective-permute-start | bytes 776 | tf_op jit(solution)/shard_map/ppermute | solution.py:59
  148.0 5.7 %collective-permute-start.3 = (f32[2,32]{1,0:T(2,128)S(1)}, f32[2,32]{1,0:T(2,128)S(1)}, u32[]{:S(2)}, u32[]{:S(2)}) collective-permute-start(f32[2,32]{1,0:T(2,128)S(1)} %collective-permute-done.2), channel_id=1, source_target_pairs={{0,2},{2,4},{4,6},{6,8},{8,10},{10,12},{12,14},{14,16},{16,18},{18... | collective-permute-start | bytes 776 | tf_op jit(solution)/shard_map/ppermute | solution.py:59
  153.7 5.7 %collective-permute-start.4 = (f32[2,32]{1,0:T(2,128)S(1)}, f32[2,32]{1,0:T(2,128)S(1)}, u32[]{:S(2)}, u32[]{:S(2)}) collective-permute-start(f32[2,32]{1,0:T(2,128)S(1)} %collective-permute-done.3), channel_id=1, source_target_pairs={{0,2},{2,4},{4,6},{6,8},{8,10},{10,12},{12,14},{14,16},{16,18},{18... | collective-permute-start | bytes 776 | tf_op jit(solution)/shard_map/ppermute | solution.py:59
  159.4 5.7 %collective-permute-start.5 = (f32[2,32]{1,0:T(2,128)S(1)}, f32[2,32]{1,0:T(2,128)S(1)}, u32[]{:S(2)}, u32[]{:S(2)}) collective-permute-start(f32[2,32]{1,0:T(2,128)S(1)} %collective-permute-done.4), channel_id=1, source_target_pairs={{0,2},{2,4},{4,6},{6,8},{8,10},{10,12},{12,14},{14,16},{16,18},{18... | collective-permute-start | bytes 776 | tf_op jit(solution)/shard_map/ppermute | solution.py:59
  165.1 5.7 %collective-permute-start.6 = (f32[2,32]{1,0:T(2,128)S(1)}, f32[2,32]{1,0:T(2,128)S(1)}, u32[]{:S(2)}, u32[]{:S(2)}) collective-permute-start(f32[2,32]{1,0:T(2,128)S(1)} %collective-permute-done.5), channel_id=1, source_target_pairs={{0,2},{2,4},{4,6},{6,8},{8,10},{10,12},{12,14},{14,16},{16,18},{18... | collective-permute-start | bytes 776 | tf_op jit(solution)/shard_map/ppermute | solution.py:59
  170.8 5.7 %collective-permute-start.7 = (f32[2,32]{1,0:T(2,128)S(1)}, f32[2,32]{1,0:T(2,128)S(1)}, u32[]{:S(2)}, u32[]{:S(2)}) collective-permute-start(f32[2,32]{1,0:T(2,128)S(1)} %collective-permute-done.6), channel_id=1, source_target_pairs={{0,2},{2,4},{4,6},{6,8},{8,10},{10,12},{12,14},{14,16},{16,18},{18... | collective-permute-start | bytes 776 | tf_op jit(solution)/shard_map/ppermute | solution.py:59
  176.5 5.7 %collective-permute-start.8 = (f32[2,32]{1,0:T(2,128)S(1)}, f32[2,32]{1,0:T(2,128)S(1)}, u32[]{:S(2)}, u32[]{:S(2)}) collective-permute-start(f32[2,32]{1,0:T(2,128)S(1)} %collective-permute-done.7), channel_id=1, source_target_pairs={{0,2},{2,4},{4,6},{6,8},{8,10},{10,12},{12,14},{14,16},{16,18},{18... | collective-permute-start | bytes 776 | tf_op jit(solution)/shard_map/ppermute | solution.py:59
  182.2 5.7 %collective-permute-start.9 = (f32[2,32]{1,0:T(2,128)S(1)}, f32[2,32]{1,0:T(2,128)S(1)}, u32[]{:S(2)}, u32[]{:S(2)}) collective-permute-start(f32[2,32]{1,0:T(2,128)S(1)} %collective-permute-done.8), channel_id=1, source_target_pairs={{0,2},{2,4},{4,6},{6,8},{8,10},{10,12},{12,14},{14,16},{16,18},{18... | collective-permute-start | bytes 776 | tf_op jit(solution)/shard_map/ppermute | solution.py:59
  187.9 5.7 %collective-permute-start.10 = (f32[2,32]{1,0:T(2,128)S(1)}, f32[2,32]{1,0:T(2,128)S(1)}, u32[]{:S(2)}, u32[]{:S(2)}) collective-permute-start(f32[2,32]{1,0:T(2,128)S(1)} %collective-permute-done.9), channel_id=1, source_target_pairs={{0,2},{2,4},{4,6},{6,8},{8,10},{10,12},{12,14},{14,16},{16,18},{18... | collective-permute-start | bytes 776 | tf_op jit(solution)/shard_map/ppermute | solution.py:59
  193.6 5.7 %collective-permute-start.11 = (f32[2,32]{1,0:T(2,128)S(1)}, f32[2,32]{1,0:T(2,128)S(1)}, u32[]{:S(2)}, u32[]{:S(2)}) collective-permute-start(f32[2,32]{1,0:T(2,128)S(1)} %collective-permute-done.10), channel_id=1, source_target_pairs={{0,2},{2,4},{4,6},{6,8},{8,10},{10,12},{12,14},{14,16},{16,18},{18... | collective-permute-start | bytes 776 | tf_op jit(solution)/shard_map/ppermute | solution.py:59
  199.3 5.7 %collective-permute-start.12 = (f32[2,32]{1,0:T(2,128)S(1)}, f32[2,32]{1,0:T(2,128)S(1)}, u32[]{:S(2)}, u32[]{:S(2)}) collective-permute-start(f32[2,32]{1,0:T(2,128)S(1)} %collective-permute-done.11), channel_id=1, source_target_pairs={{0,2},{2,4},{4,6},{6,8},{8,10},{10,12},{12,14},{14,16},{16,18},{18... | collective-permute-start | bytes 776 | tf_op jit(solution)/shard_map/ppermute | solution.py:59
  205.0 5.7 %collective-permute-start.13 = (f32[2,32]{1,0:T(2,128)S(1)}, f32[2,32]{1,0:T(2,128)S(1)}, u32[]{:S(2)}, u32[]{:S(2)}) collective-permute-start(f32[2,32]{1,0:T(2,128)S(1)} %collective-permute-done.12), channel_id=1, source_target_pairs={{0,2},{2,4},{4,6},{6,8},{8,10},{10,12},{12,14},{14,16},{16,18},{18... | collective-permute-start | bytes 776 | tf_op jit(solution)/shard_map/ppermute | solution.py:59
  210.7 5.7 %collective-permute-start.14 = (f32[2,32]{1,0:T(2,128)S(1)}, f32[2,32]{1,0:T(2,128)S(1)}, u32[]{:S(2)}, u32[]{:S(2)}) collective-permute-start(f32[2,32]{1,0:T(2,128)S(1)} %collective-permute-done.13), channel_id=1, source_target_pairs={{0,2},{2,4},{4,6},{6,8},{8,10},{10,12},{12,14},{14,16},{16,18},{18... | collective-permute-start | bytes 776 | tf_op jit(solution)/shard_map/ppermute | solution.py:59
  217.5 16.2 %copy-start.1 = (s32[32,8]{0,1:T(8,128)S(1)}, s32[32,8]{0,1:T(8,128)}, u32[]{:S(2)}) copy-start(s32[32,8]{0,1:T(8,128)} %param.9) | copy-start | bytes 3076
Sparse Core Ops, SparseCore 0:
  233.8 23.0 all-reduce.2
